TPU v7x, 32 devices: a whole 2x2x4 slice. The times are simulated.
32 devices in a mesh: space: 2 (over x), vel: 16 (over z, y, core).
Axes of the slice: x: 2, y: 2, z: 4, core: 2. Of those that a mesh axis runs over, the one named last changes fastest.
Arguments:
- distribution: float32 [8192, 512], P('vel', 'space'), may hold values from 0.1 to 32, as said below
- normals: float32 [4, 3, 512], P(None, None, 'space'), may hold values from -0.3 to 0.3
- adjacency: int32 [4, 512], P(None, 'space'), may hold values from 0 to 511, as said below
- send_list: int32 [2, 2, 256], P('space'), may hold values from 0 to 255
- block_counts: int32 [2, 2], P(None, 'space'), may hold values from 0 to 2, as said below
Outputs:
- relaxed: float32 [8192, 512], P('vel', 'space')
- fields: float32 [13, 512], P(None, 'space')
Inputs may be any that keep to these rules, and one draw needn't show every extreme that they name: `adjacency`: every entry of 256 or more names a position below 128 times the sum of block_counts over the senders to its group. `block_counts`: no group sends to itself; every other pair has at least one block; one receiving group gets 2 blocks from every other group. `distribution`: Positive.
All inputs are finite; a program needn't handle non-finite values.
Results may differ from a plain program's by a relative error of at most 0.00011.
Values sent between devices are 32-bit elements; how exact they have to be, the bound alone decides.
A program may use at most 64 MiB of HBM per device.

v0:
```python
import jax
import jax.numpy as jnp
from jax import lax
from jax.sharding import PartitionSpec as P

VXY = 32
TILE = 128
ITERS = 2
spacing = 0.3
ellipsoid_mix = -0.25
prandtl = 0.8
visc_power = 0.26
time_step = 0.025


def velocity_nodes(vel_index, z_count):
    comp_x = (vel_index % VXY).astype(jnp.float32)
    comp_y = (vel_index // VXY % VXY).astype(jnp.float32)
    comp_z = (vel_index // (VXY * VXY)).astype(jnp.float32)
    centre = (VXY - 1) / 2.0
    return jnp.stack(
        [
            (comp_x - centre) * spacing,
            (comp_y - centre) * spacing,
            (comp_z - (z_count - 1) / 2.0) * spacing,
        ]
    )


def moment_rows(velocity):
    comp_x, comp_y, comp_z = (velocity[0], velocity[1], velocity[2])
    squared = comp_x * comp_x + comp_y * comp_y + comp_z * comp_z
    return jnp.stack(
        [
            jnp.ones_like(comp_x),
            comp_x,
            comp_y,
            comp_z,
            comp_x * comp_x,
            comp_y * comp_y,
            comp_z * comp_z,
            comp_x * comp_y,
            comp_x * comp_z,
            comp_y * comp_z,
            comp_x * squared,
            comp_y * squared,
            comp_z * squared,
        ]
    )


def quad_rows(velocity):
    comp_x, comp_y, comp_z = (velocity[0], velocity[1], velocity[2])
    return jnp.stack(
        [
            comp_x * comp_x,
            comp_y * comp_y,
            comp_z * comp_z,
            comp_x * comp_y,
            comp_x * comp_z,
            comp_y * comp_z,
            comp_x,
            comp_y,
            comp_z,
            jnp.ones_like(comp_x),
        ]
    )


def macroscopic(moments):
    density = moments[0]
    mean_x = moments[1] / density
    mean_y = moments[2] / density
    mean_z = moments[3] / density
    second = moments[4:10] / density[None, :]
    third = moments[10:13] / density[None, :]
    theta_xx = second[0] - mean_x * mean_x
    theta_yy = second[1] - mean_y * mean_y
    theta_zz = second[2] - mean_z * mean_z
    theta_xy = second[3] - mean_x * mean_y
    theta_xz = second[4] - mean_x * mean_z
    theta_yz = second[5] - mean_y * mean_z
    temper = (theta_xx + theta_yy + theta_zz) / 3.0
    trace_b = second[0] + second[1] + second[2]
    bu_x = second[0] * mean_x + second[3] * mean_y + second[4] * mean_z
    bu_y = second[3] * mean_x + second[1] * mean_y + second[5] * mean_z
    bu_z = second[4] * mean_x + second[5] * mean_y + second[2] * mean_z
    mean_sq = mean_x * mean_x + mean_y * mean_y + mean_z * mean_z
    flux_x = 0.5 * (third[0] - 2.0 * bu_x - mean_x * trace_b + 2.0 * mean_x * mean_sq)
    flux_y = 0.5 * (third[1] - 2.0 * bu_y - mean_y * trace_b + 2.0 * mean_y * mean_sq)
    flux_z = 0.5 * (third[2] - 2.0 * bu_z - mean_z * trace_b + 2.0 * mean_z * mean_sq)
    iso_part = (1.0 - ellipsoid_mix) * temper
    lam_xx = iso_part + ellipsoid_mix * theta_xx
    lam_yy = iso_part + ellipsoid_mix * theta_yy
    lam_zz = iso_part + ellipsoid_mix * theta_zz
    lam_xy = ellipsoid_mix * theta_xy
    lam_xz = ellipsoid_mix * theta_xz
    lam_yz = ellipsoid_mix * theta_yz
    cof_xx = lam_yy * lam_zz - lam_yz * lam_yz
    cof_xy = lam_yz * lam_xz - lam_xy * lam_zz
    cof_xz = lam_xy * lam_yz - lam_yy * lam_xz
    cof_yy = lam_xx * lam_zz - lam_xz * lam_xz
    cof_yz = lam_xy * lam_xz - lam_xx * lam_yz
    cof_zz = lam_xx * lam_yy - lam_xy * lam_xy
    determinant = lam_xx * cof_xx + lam_xy * cof_xy + lam_xz * cof_xz
    inv_xx = cof_xx / determinant
    inv_yy = cof_yy / determinant
    inv_zz = cof_zz / determinant
    inv_xy = cof_xy / determinant
    inv_xz = cof_xz / determinant
    inv_yz = cof_yz / determinant
    lin_x = inv_xx * mean_x + inv_xy * mean_y + inv_xz * mean_z
    lin_y = inv_xy * mean_x + inv_yy * mean_y + inv_yz * mean_z
    lin_z = inv_xz * mean_x + inv_yz * mean_y + inv_zz * mean_z
    offset = mean_x * lin_x + mean_y * lin_y + mean_z * lin_z
    collide = prandtl * density * jnp.exp(visc_power * jnp.log(temper))
    return jnp.stack(
        [
            density,
            mean_x,
            mean_y,
            mean_z,
            theta_xx,
            theta_yy,
            theta_zz,
            theta_xy,
            theta_xz,
            theta_yz,
            flux_x,
            flux_y,
            flux_z,
            inv_xx,
            inv_yy,
            inv_zz,
            2.0 * inv_xy,
            2.0 * inv_xz,
            2.0 * inv_yz,
            -2.0 * lin_x,
            -2.0 * lin_y,
            -2.0 * lin_z,
            offset,
            collide,
        ]
    )


def ghost_slots(adjacency, counts, cells, groups, slot_count):
    ends = jnp.cumsum(counts) * TILE
    starts = ends - counts * TILE
    is_local = adjacency < cells
    position = jnp.maximum(adjacency - cells, 0)
    source = jnp.sum((ends[:, None, None] <= position[None]).astype(jnp.int32), axis=0)
    source = jnp.minimum(source, groups - 1)
    group_ids = jnp.arange(groups, dtype=jnp.int32)[:, None, None]
    chosen = jnp.sum(jnp.where(group_ids == source[None], starts[:, None, None], 0), axis=0)
    slot_pos = jnp.clip(position - chosen, 0, slot_count - 1)
    return (is_local, source, slot_pos)


def relax(current, neighbours, velocity, normals, params, norm_z, equilibrium):
    gauss = params[0][None, :] * equilibrium / norm_z[None, :]
    outflow = jnp.zeros(current.shape, jnp.float32)
    inflow = jnp.zeros(current.shape, jnp.float32)
    for side in range(normals.shape[0]):
        normal_speed = (
            velocity[0][:, None] * normals[side, 0][None, :]
            + velocity[1][:, None] * normals[side, 1][None, :]
            + velocity[2][:, None] * normals[side, 2][None, :]
        )
        outflow = outflow + jnp.maximum(normal_speed, 0.0)
        inflow = inflow + jnp.minimum(normal_speed, 0.0) * neighbours[side]
    return current + time_step * (
        params[23][None, :] * (gauss - current) - outflow * current - inflow
    )


def per_device(distribution, normals, adjacency, send_list, block_counts):
    vel_local = distribution.shape[0]
    cells = distribution.shape[1]
    total_vel = vel_local * lax.axis_size("vel")
    z_count = total_vel // (VXY * VXY)
    groups = send_list.shape[1]
    slot_count = send_list.shape[2]
    vel_index = lax.axis_index("vel") * vel_local + jnp.arange(vel_local, dtype=jnp.int32)
    velocity = velocity_nodes(vel_index, z_count)
    moment_table = moment_rows(velocity)
    quad_table = quad_rows(velocity).T
    is_local, source, slot_pos = ghost_slots(
        adjacency, block_counts[:, 0], cells, groups, slot_count
    )
    ghost_index = source * slot_count + slot_pos
    local_index = jnp.where(is_local, adjacency, 0)
    send_rows = send_list[0].reshape(-1)

    def reduce_moments(current):
        partial_value = (
            jnp.dot(
                moment_table,
                current,
                precision=lax.Precision.HIGHEST,
                preferred_element_type=jnp.float32,
            )
            / total_vel
        )
        return macroscopic(lax.psum(partial_value, "vel"))

    current = distribution
    for iteration in range(ITERS):
        params = reduce_moments(current)
        ghosts = lax.all_to_all(
            jnp.take(current, send_rows, axis=1), "space", split_axis=1, concat_axis=1, tiled=True
        )
        exponent = jnp.dot(
            quad_table,
            params[13:23],
            precision=lax.Precision.HIGHEST,
            preferred_element_type=jnp.float32,
        )
        equilibrium = jnp.exp(-0.5 * exponent)
        norm_z = lax.psum(jnp.sum(equilibrium, axis=0) / total_vel, "vel")
        neighbours = [
            jnp.where(
                is_local[side][None, :],
                jnp.take(current, local_index[side], axis=1),
                jnp.take(ghosts, ghost_index[side], axis=1),
            )
            for side in range(normals.shape[0])
        ]
        current = relax(current, neighbours, velocity, normals, params, norm_z, equilibrium)
    final = reduce_moments(current)
    return (current, final[:13])


def solution(mesh):
    placed = (
        P("vel", "space"),
        P(None, None, "space"),
        P(None, "space"),
        P("space", None, None),
        P(None, "space"),
    )
    return jax.shard_map(
        per_device,
        mesh=mesh,
        in_specs=placed,
        out_specs=(P("vel", "space"), P(None, "space")),
        check_vma=False,
    )
```

profile of v0, /device:TPU:0, one launch (start us, length us, event | category | flops | bytes accessed | tf_op | source)
XLA Modules:
  0.0 309.6 jit_solution(3086310342836148335)
XLA Ops:
  1.3 1.2 copy.33
  2.6 1.6 gather_fusion.1
  4.2 1.1 broadcast_select_fusion.1
  5.4 4.4 %all-to-all-start = ((f32[512,2,256]{0,2,1:T(8,128)}), f32[512,2,256]{0,2,1:T(8,128)S(1)}, u32[]{:S(2)}, u32[]{:S(2)}) async-start(f32[512,2,256]{0,2,1:T(8,128)} %bitcast.20), calls=%async_computation | async-start | bytes 2097152 | tf_op jit(solution)/shard_map/all_to_all | solution.py:210
  11.7 62.4 %psum.35 = f32[13,256]{1,0:T(8,128)S(1)} all-reduce(f32[13,256]{1,0:T(8,128)S(1)} %convolution_multiply_fusion.4), channel_id=1, replica_groups=mesh['space'=2,'vel'=16] {'vel'}, use_global_device_ids=true, to_apply=%region_0.1 | all-reduce | flops 3328 | bytes 26624 | tf_op jit(solution)/shard_map/psum | solution.py:205
  74.9 29.5 %psum.36 = f32[256]{0:T(256)S(1)} all-reduce(f32[256]{0:T(256)S(1)} %broadcast_multiply_fusion.1), channel_id=1, replica_groups=mesh['space'=2,'vel'=16] {'vel'}, use_global_device_ids=true, to_apply=%region_2.3 | all-reduce | flops 256 | bytes 2048 | tf_op jit(solution)/shard_map/psum | solution.py:220
  104.5 1.8 gather_fusion
  106.2 1.2 copy.34
  107.5 1.8 gather_fusion.3
  109.3 2.0 copy.38
  111.3 1.8 gather_fusion.5
  113.1 2.1 copy.41
  115.1 1.8 gather_fusion.7
  116.9 2.1 copy.44
  125.0 1.8 gather_fusion.8
  126.7 2.1 copy.45
  128.9 2.9 fusion.16
  132.3 57.6 %psum.37 = f32[13,256]{1,0:T(8,128)S(1)} all-reduce(f32[13,256]{1,0:T(8,128)S(1)} %convolution_multiply_fusion.3), channel_id=1, replica_groups=mesh['space'=2,'vel'=16] {'vel'}, use_global_device_ids=true, to_apply=%region_6.10 | all-reduce | flops 3328 | bytes 26624 | tf_op jit(solution)/shard_map/psum | solution.py:205
  190.1 1.6 gather_fusion.10
  191.7 1.1 broadcast_select_fusion
  192.9 3.8 %all-to-all-start.1 = ((f32[512,2,256]{0,2,1:T(8,128)}), f32[512,2,256]{0,2,1:T(8,128)S(1)}, u32[]{:S(2)}, u32[]{:S(2)}) async-start(f32[512,2,256]{0,2,1:T(8,128)} %bitcast.39), calls=%async_computation.1 | async-start | bytes 2097152 | tf_op jit(solution)/shard_map/all_to_all | solution.py:210
  198.6 1.8 gather_fusion.14
  200.4 1.8 gather_fusion.16
  202.6 2.1 copy.54
  205.7 1.4 fusion.95
  207.2 29.5 %psum.38 = f32[256]{0:T(256)S(1)} all-reduce(f32[256]{0:T(256)S(1)} %broadcast_multiply_fusion), channel_id=1, replica_groups=mesh['space'=2,'vel'=16] {'vel'}, use_global_device_ids=true, to_apply=%region_8.12 | all-reduce | flops 256 | bytes 2048 | tf_op jit(solution)/shard_map/psum | solution.py:220
  237.6 1.8 gather_fusion.13
  239.4 1.8 gather_fusion.15
  241.2 1.8 gather_fusion.17
  247.4 2.9 fusion.6
  250.7 57.7 %psum.39 = f32[13,256]{1,0:T(8,128)S(1)} all-reduce(f32[13,256]{1,0:T(8,128)S(1)} %convolution_multiply_fusion.2), channel_id=1, replica_groups=mesh['space'=2,'vel'=16] {'vel'}, use_global_device_ids=true, to_apply=%region_9.13 | all-reduce | flops 3328 | bytes 26624 | tf_op jit(solution)/shard_map/psum | solution.py:205
  308.4 1.2 stack.14
  (131 shorter events, 19.2 us)
Async XLA Ops:
  5.3 6.0 %copy-start = (f32[512,256]{1,0:T(8,128)S(1)}, f32[512,256]{1,0:T(8,128)}, u32[]{:S(2)}) copy-start(f32[512,256]{1,0:T(8,128)} %param.11) | copy-start | bytes 1572868
  5.4 113.7 %all-to-all-start = ((f32[512,2,256]{0,2,1:T(8,128)}), f32[512,2,256]{0,2,1:T(8,128)S(1)}, u32[]{:S(2)}, u32[]{:S(2)}) async-start(f32[512,2,256]{0,2,1:T(8,128)} %bitcast.20), calls=%async_computation | async-start | bytes 2097152 | tf_op jit(solution)/shard_map/all_to_all | solution.py:210
  10.0 0.7 copy-start.12
  10.0 0.8 copy-start.10
  116.9 2.1 copy-start.11
  126.7 2.1 copy-start.4
  126.7 2.1 copy-start.5
  192.9 43.8 %all-to-all-start.1 = ((f32[512,2,256]{0,2,1:T(8,128)}), f32[512,2,256]{0,2,1:T(8,128)S(1)}, u32[]{:S(2)}, u32[]{:S(2)}) async-start(f32[512,2,256]{0,2,1:T(8,128)} %bitcast.39), calls=%async_computation.1 | async-start | bytes 2097152 | tf_op jit(solution)/shard_map/all_to_all | solution.py:210
  202.5 2.1 copy-start.6
  242.9 1.0 copy-start.7
  244.0 1.0 copy-start.8
  245.0 1.0 copy-start.9
  246.1 1.0 copy-start.2
  246.1 1.4 copy-start.3
  250.4 59.3 %copy-start.1 = (f32[512,256]{1,0:T(8,128)}, f32[512,256]{1,0:T(8,128)S(1)}, u32[]{:S(2)}) copy-start(f32[512,256]{1,0:T(8,128)S(1)} %fusion.6) | copy-start | bytes 1572868
where the time goes:
time: 311 us; the launch traced here: 310 us
  blocking collectives  237 us (76%)
  local copies, waits for them, and re-layouts  51.6 us (17%)
  other arithmetic  9.24 us (3%)
  starting transfers between devices  8.12 us (3%)
    psum x3, blocking collectives, reduce_moments(): return macroscopic(lax.psum(partial_value, 'vel'))  178 us
    psum x2, blocking collectives, per_device(): norm_z = lax.psum(jnp.sum(equilibrium, axis=0) / total_vel, 'vel')  59 us
    gather x16, local copies, waits for them, and re-layouts, per_device(): jnp.take(current, local_index[side], axis=1)  23.4 us
    gather x16, local copies, waits for them, and re-layouts, per_device(): jnp.take(ghosts, ghost_index[side], axis=1)  20.1 us
    all_to_all x2, starting transfers between devices, per_device(): lax.all_to_all(jnp.take(current, send_rows, axis=1), 'space', split_axis=...  8.12 us
  transfers between devices with their start and end apart: 2, of which 0 were waited for; matrix products, arithmetic and copies ran while one was open for 9% of the time, Pallas kernels for 0%

commit v1 on v0

--- a/solution.py
+++ b/solution.py
@@ -217,7 +217,7 @@
             preferred_element_type=jnp.float32,
         )
         equilibrium = jnp.exp(-0.5 * exponent)
-        norm_z = lax.psum(jnp.sum(equilibrium, axis=0) / total_vel, "vel")
+        norm_z = jnp.sum(lax.all_gather(jnp.sum(equilibrium, axis=0) / total_vel, "vel"), axis=0)
         neighbours = [
             jnp.where(
                 is_local[side][None, :],

time: 311 us -> 294 us (0.945)
  blocking collectives: 237 us -> 216 us
  local copies, waits for them, and re-layouts: 51.6 us -> 56.3 us
    psum x2 -> x0, blocking collectives: 59 us -> none  [per_device(): norm_z = lax.psum(jnp.sum(equilibrium, axis=0) / total_vel, 'vel')]
    all_gather x0 -> x2, blocking collectives: none -> 34.3 us  [per_device(): lax.all_gather(jnp.sum(equilibrium, axis=0) / total_vel, 'vel')]
    psum x3, blocking collectives: 178 us -> 181 us  [reduce_moments(): return macroscopic(lax.psum(partial_value, 'vel'))]
    gather x16, local copies, waits for them, and re-layouts: 23.4 us -> 26.8 us  [per_device(): jnp.take(current, local_index[side], axis=1)]
  transfers between devices with their start and end apart: 2 -> 2, of which waited for: 0 -> 0; matrix products, arithmetic and copies ran while one was open for 9% -> 10% of each run, Pallas kernels for 0% -> 0%
where the time goes in v1:
time: 294 us; the launch traced here: 293 us
  blocking collectives  216 us (73%)
  local copies, waits for them, and re-layouts  56.3 us (19%)
  other arithmetic  9.31 us (3%)
  starting transfers between devices  8.12 us (3%)
    psum x3, blocking collectives, reduce_moments(): return macroscopic(lax.psum(partial_value, 'vel'))  181 us
    all_gather x2, blocking collectives, per_device(): lax.all_gather(jnp.sum(equilibrium, axis=0) / total_vel, 'vel')  34.3 us
    gather x16, local copies, waits for them, and re-layouts, per_device(): jnp.take(current, local_index[side], axis=1)  26.8 us
    gather x16, local copies, waits for them, and re-layouts, per_device(): jnp.take(ghosts, ghost_index[side], axis=1)  21.2 us
    all_to_all x2, starting transfers between devices, per_device(): lax.all_to_all(jnp.take(current, send_rows, axis=1), 'space', split_axis=...  8.12 us
  transfers between devices with their start and end apart: 2, of which 0 were waited for; matrix products, arithmetic and copies ran while one was open for 10% of the time, Pallas kernels for 0%

profile of v1, /device:TPU:0, one launch (start us, length us, event | category | flops | bytes accessed | tf_op | source)
XLA Modules:
  0.0 292.7 jit_solution(5374716571696782291)
XLA Ops:
  1.3 1.2 copy.59
  2.6 1.6 gather_fusion.1
  5.4 4.4 %all-to-all-start = ((f32[512,2,256]{0,2,1:T(8,128)}), f32[512,2,256]{0,2,1:T(8,128)S(1)}, u32[]{:S(2)}, u32[]{:S(2)}) async-start(f32[512,2,256]{0,2,1:T(8,128)} %bitcast.21), calls=%async_computation | async-start | bytes 2097152 | tf_op jit(solution)/shard_map/all_to_all | solution.py:210
  11.7 62.4 %psum.21 = f32[13,256]{1,0:T(8,128)S(1)} all-reduce(f32[13,256]{1,0:T(8,128)S(1)} %convolution_multiply_fusion.4), channel_id=1, replica_groups=mesh['space'=2,'vel'=16] {'vel'}, use_global_device_ids=true, to_apply=%region_0.1 | all-reduce | flops 3328 | bytes 26624 | tf_op jit(solution)/shard_map/psum | solution.py:205
  74.9 17.2 %all-gather.2 = f32[16,1,256]{2,1,0:T(1,128)S(1)} all-gather(f32[1,1,256]{2,1,0:T(1,128)S(1)} %bitcast.195), channel_id=2, replica_groups=mesh['space'=2,'vel'=16] {'vel'}, dimensions={0}, use_global_device_ids=true | all-gather | bytes 17408 | tf_op jit(solution)/shard_map/all_gather | solution.py:220
  92.2 1.8 gather_fusion
  95.2 1.8 gather_fusion.3
  96.9 2.0 copy.64
  99.0 1.8 gather_fusion.5
  100.7 2.1 copy.67
  102.8 1.8 gather_fusion.7
  104.6 2.1 copy.70
  113.3 1.8 gather_fusion.8
  115.1 2.1 copy.71
  117.2 2.9 %fusion.16 = f32[512,256]{1,0:T(8,128)S(1)} fusion(f32[512,256]{1,0:T(8,128)S(1)} %copy-done, f32[256,512]{0,1:T(8,128)} %copy.71, f32[256,512]{0,1:T(8,128)} %copy.70, f32[256,512]{0,1:T(8,128)} %copy.68, f32[256,512]{0,1:T(8,128)S(1)} %copy-done.5, f32[256,512]{0,1:T(8,128)} %copy.65, f32[256,512]{0,1:T(8,128)S(1)} %copy-done.2, f32[256,512]{0,1:T(8,128)} %copy.62, ...), kind=kLoop, calls=%fused_computation.44 | loop fusion | flops 7733248 | bytes 5791744 | tf_op jit(solution)/shard_map/add | solution.py:172
  120.7 59.4 %psum.22 = f32[13,256]{1,0:T(8,128)S(1)} all-reduce(f32[13,256]{1,0:T(8,128)S(1)} %convolution_multiply_fusion.3), channel_id=1, replica_groups=mesh['space'=2,'vel'=16] {'vel'}, use_global_device_ids=true, to_apply=%region_6.10 | all-reduce | flops 3328 | bytes 26624 | tf_op jit(solution)/shard_map/psum | solution.py:205
  180.3 1.6 gather_fusion.10
  183.0 3.8 %all-to-all-start.1 = ((f32[512,2,256]{0,2,1:T(8,128)}), f32[512,2,256]{0,2,1:T(8,128)S(1)}, u32[]{:S(2)}, u32[]{:S(2)}) async-start(f32[512,2,256]{0,2,1:T(8,128)} %bitcast.41), calls=%async_computation.1 | async-start | bytes 2097152 | tf_op jit(solution)/shard_map/all_to_all | solution.py:210
  186.8 1.8 gather_fusion.9
  188.6 1.8 gather_fusion.12
  190.3 1.8 gather_fusion.14
  192.1 1.8 gather_fusion.16
  194.6 17.2 %all-gather.3 = f32[16,1,256]{2,1,0:T(1,128)S(1)} all-gather(f32[1,1,256]{2,1,0:T(1,128)S(1)} %bitcast.196), channel_id=3, replica_groups=mesh['space'=2,'vel'=16] {'vel'}, dimensions={0}, use_global_device_ids=true | all-gather | bytes 17408 | tf_op jit(solution)/shard_map/all_gather | solution.py:220
  212.0 2.1 copy.77
  215.1 2.1 copy.83
  218.2 1.8 gather_fusion.13
  219.9 1.8 gather_fusion.15
  221.7 1.8 gather_fusion.17
  226.5 2.1 copy.84
  228.7 2.9 %fusion.6 = f32[512,256]{1,0:T(8,128)S(1)} fusion(f32[512,256]{1,0:T(8,128)S(1)} %fusion.16, f32[256,512]{0,1:T(8,128)} %copy.84, f32[256,512]{0,1:T(8,128)} %copy.83, f32[256,512]{0,1:T(8,128)} %copy.81, f32[256,512]{0,1:T(8,128)S(1)} %copy-done.4, f32[256,512]{0,1:T(8,128)} %copy.78, f32[256,512]{0,1:T(8,128)S(1)} %copy-done.3, f32[256,512]{0,1:T(8,128)} %copy.75, ...), kind=kLoop, calls=%fused_computation.30 | loop fusion | flops 7733248 | bytes 5791744 | tf_op jit(solution)/shard_map/add | solution.py:172
  231.9 59.5 %psum.23 = f32[13,256]{1,0:T(8,128)S(1)} all-reduce(f32[13,256]{1,0:T(8,128)S(1)} %convolution_multiply_fusion.2), channel_id=1, replica_groups=mesh['space'=2,'vel'=16] {'vel'}, use_global_device_ids=true, to_apply=%region_9.13 | all-reduce | flops 3328 | bytes 26624 | tf_op jit(solution)/shard_map/psum | solution.py:205
  291.5 1.2 stack.14
  (133 shorter events, 20.5 us)
Async XLA Ops:
  5.3 6.0 %copy-start = (f32[512,256]{1,0:T(8,128)S(1)}, f32[512,256]{1,0:T(8,128)}, u32[]{:S(2)}) copy-start(f32[512,256]{1,0:T(8,128)} %param.11) | copy-start | bytes 1572868
  5.4 102.0 %all-to-all-start = ((f32[512,2,256]{0,2,1:T(8,128)}), f32[512,2,256]{0,2,1:T(8,128)S(1)}, u32[]{:S(2)}, u32[]{:S(2)}) async-start(f32[512,2,256]{0,2,1:T(8,128)} %bitcast.21), calls=%async_computation | async-start | bytes 2097152 | tf_op jit(solution)/shard_map/all_to_all | solution.py:210
  10.0 0.7 copy-start.12
  10.0 0.8 copy-start.10
  106.6 0.7 copy-start.11
  115.1 2.1 copy-start.2
  115.1 2.1 copy-start.5
  183.0 34.2 %all-to-all-start.1 = ((f32[512,2,256]{0,2,1:T(8,128)}), f32[512,2,256]{0,2,1:T(8,128)S(1)}, u32[]{:S(2)}, u32[]{:S(2)}) async-start(f32[512,2,256]{0,2,1:T(8,128)} %bitcast.41), calls=%async_computation.1 | async-start | bytes 2097152 | tf_op jit(solution)/shard_map/all_to_all | solution.py:210
  193.9 17.9 %copy-start.6 = (f32[256,512]{1,0:T(8,128)S(1)}, f32[256,512]{1,0:T(8,128)}, u32[]{:S(2)}) copy-start(f32[256,512]{1,0:T(8,128)} %gather_fusion.9) | copy-start | bytes 1572868
  212.0 2.1 copy-start.7
  223.5 1.0 copy-start.8
  224.5 1.0 copy-start.9
  226.5 2.1 copy-start.3
  226.5 2.1 copy-start.4
  231.6 61.1 %copy-start.1 = (f32[512,256]{1,0:T(8,128)}, f32[512,256]{1,0:T(8,128)S(1)}, u32[]{:S(2)}) copy-start(f32[512,256]{1,0:T(8,128)S(1)} %fusion.6) | copy-start | bytes 1572868
